TPU v7x, 512 devices: a whole 4x8x8 slice. The times are simulated.
512 devices in a mesh: row: 32 (over y, x_hi, core), col: 16 (over z, x_lo).
Axes of the slice: x: 4 (x_hi: 2, x_lo: 2; x = x_hi * 2 + x_lo), y: 8, z: 8, core: 2. Of those that a mesh axis runs over, the one named last changes fastest.
Arguments:
- temps: bfloat16 [12, 64, 262144], P(None, None, ('row', 'col')), may hold values from -6 to 6
- sensors: int32 [12, 2048], replicated, may hold values from 0 to 262143
Outputs:
- corr: bfloat16 [2048, 262144], P('col', 'row')
Inputs may be any that keep to these rules, and one draw needn't show every extreme that they name: `sensors`: each entry is a pixel index of its tier; candidates may repeat.
All inputs are finite; a program needn't handle non-finite values.
Results may differ from a plain program's by a relative error of at most 0.001.
Values may be sent and summed in bfloat16 or wider, within the bound.
No kernel may reach another device: no remote copies, remote signals or barrier semaphores. Data moves between devices by JAX's collectives and lax.ppermute only.
A program may use at most 64 MiB of HBM per device.

v0:
```python
import jax
import jax.numpy as jnp
from jax import lax
from jax.sharding import Mesh
from jax.sharding import PartitionSpec as P

COL = ("col_0", "col_1")
ROW_COL = ("row", "col_0", "col_1")


def scatter_axes(value, axes, dim):
    for axis in axes:
        value = lax.psum_scatter(value, axis, scatter_dimension=dim, tiled=True)
    return value


def filled_up(lines, length):
    spare = -lines.shape[0] % length
    if not spare:
        return lines
    return jnp.concatenate([lines, jnp.zeros((spare, *lines.shape[1:]), lines.dtype)])


def sent_to_all(value, axis):
    length = lax.axis_size(axis)
    return lax.all_to_all(
        jnp.broadcast_to(value[None], (length, *value.shape)), axis, 0, 0, tiled=True
    )


def laid_out(blocks, dim):
    blocks = jnp.moveaxis(blocks, 0, dim)
    shape = blocks.shape
    return blocks.reshape(*shape[:dim], shape[dim] * shape[dim + 1], *shape[dim + 2 :])


def gather_directly(value, axis, dim):
    blocks = sent_to_all(value, axis)
    return laid_out(blocks, dim)


def in_blocks(value, dim, length):
    before, after = (value.shape[:dim], value.shape[dim + 1 :])
    return jnp.moveaxis(value.reshape(*before, length, -1, *after), dim, 0)


def sent_and_summed(value, axis, dim):
    blocks = in_blocks(value, dim, lax.axis_size(axis))
    arrived = lax.all_to_all(blocks, axis, split_axis=0, concat_axis=0, tiled=True)
    return arrived.astype(jnp.float32).sum(axis=0)


def total_of(value, axes):
    lines = value.reshape(-1, value.shape[-1])
    padded = filled_up(lines, lax.axis_size(axes))
    whole = gather_directly(sent_and_summed(padded, axes, 0).astype(jnp.bfloat16), axes, 0)
    return lax.slice_in_dim(whole, 0, len(lines)).reshape(value.shape).astype(jnp.float32)


def select_columns(fields, sensor_rows, first_pixel):
    width = fields.shape[2]
    offsets = sensor_rows - first_pixel
    pixel_ids = lax.broadcasted_iota(jnp.int32, (width, sensor_rows.shape[1]), 0)

    def one_tier(pair):
        tier_fields, tier_offsets = pair
        selector = (pixel_ids == tier_offsets[None, :]).astype(jnp.bfloat16)
        return jnp.dot(tier_fields, selector, preferred_element_type=jnp.float32)

    return lax.map(one_tier, (fields, offsets))


def body(temps, sensors):
    col_count = lax.axis_size(COL)
    first_pixel = (lax.axis_index("row") * col_count + lax.axis_index(COL)) * temps.shape[2]
    local_values = select_columns(temps, sensors, first_pixel)
    owned = (
        scatter_axes(local_values.astype(jnp.bfloat16), COL, 2)
        .astype(jnp.float32)
        .astype(jnp.bfloat16)
    )
    readings = total_of(owned, "row").astype(jnp.bfloat16)
    scale_factor = 1.0 / jnp.sqrt(jnp.float32(temps.shape[0] * temps.shape[1]))
    summed = jnp.einsum(
        "tsc,tsp->cp",
        lax.all_gather(readings, COL, axis=2, tiled=True),
        temps,
        preferred_element_type=jnp.float32,
    )
    rounded = (summed * scale_factor).astype(jnp.bfloat16)
    return lax.all_to_all(rounded, COL, split_axis=0, concat_axis=1, tiled=True)


def solution(mesh):
    torus = Mesh(mesh.devices.reshape(mesh.shape["row"], 8, 2), ("row", "col_0", "col_1"))
    in_specs = (P(None, None, ROW_COL), P())
    out_specs = P(COL, "row")
    return jax.shard_map(body, mesh=torus, in_specs=in_specs, out_specs=out_specs, check_vma=False)
```

profile of v0, /device:TPU:4, one launch (start us, length us, event | category | flops | bytes accessed | tf_op | source)
XLA Modules:
  0.0 315.9 jit_solution(11540507424467396206)
XLA Ops:
  6.5 0.0 reduce-scatter.5.cloned.1.call-start
  6.5 0.9 broadcast_subtract_fusion
  7.5 29.6 %while.11 = (s32[]{:T(128)}, bf16[12,64,2048]{2,1,0:T(8,128)(2,1)}, bf16[12,64,512]{2,1,0:T(8,128)(2,1)}, s32[12,2048]{1,0:T(8,128)S(1)}, s32[]{:T(128)}) while((s32[]{:T(128)}, bf16[12,64,2048]{2,1,0:T(8,128)(2,1)}, bf16[12,64,512]{2,1,0:T(8,128)(2,1)}, s32[12,2048]{1,0:T(8,128)S(1)}, s32[]{:T(128)}) %tuple.21), condition=%wide.region_1.2_spmd.clone, body=%wide.region_0.1_spmd.clone.sunk | while | flops 135266304 | bytes 615489 | solution.py:70
  7.5 2.4 fusion.15
  9.9 2.5 fusion.15
  12.4 2.4 fusion.15
  14.9 2.5 fusion.15
  17.3 2.5 fusion.15
  19.8 2.5 fusion.15
  22.3 2.5 fusion.15
  24.7 2.4 fusion.15
  27.2 2.5 fusion.15
  29.7 2.5 fusion.15
  32.2 2.5 fusion.15
  34.6 2.5 fusion.15
  37.1 0.0 reduce-scatter.5.cloned.1.call-update
  37.1 0.0 copy-start
  37.1 0.0 reduce-scatter.7.cloned.1.call-start
  37.2 54.7 %reduce-scatter.5.cloned.1.call-done = bf16[12,64,256]{2,1,0:T(8,128)(2,1)} async-done(((bf16[12,64,2048]{2,1,0:T(8,128)(2,1)}), bf16[12,64,256]{2,1,0:T(8,128)(2,1)}) %reduce-scatter.5.cloned.1.call-update) | async-done | bytes 393232 | tf_op jit(solution)/shard_map/reduce_scatter | solution.py:13
  91.9 1.9 copy.5
  93.8 1.4 reshape.5
  95.2 0.0 reduce-scatter.7.cloned.1.call-update
  95.2 0.0 all-gather.2.cloned.1.call-start
  95.3 19.6 %reduce-scatter.7.cloned.1.call-done = bf16[128,768]{1,0:T(8,128)(2,1)} async-done(((bf16[256,768]{1,0:T(8,128)(2,1)}), bf16[128,768]{1,0:T(8,128)(2,1)}) %reduce-scatter.7.cloned.1.call-update) | async-done | bytes 196624
  114.9 1.3 reshape.6
  116.2 0.4 copy.6
  116.6 20.3 %all_to_all.29 = bf16[32,24,128]{2,1,0:T(8,128)(2,1)S(1)} all-to-all(bf16[32,24,128]{2,1,0:T(8,128)(2,1)S(1)} %bitcast.33), channel_id=1, replica_groups=mesh['row'=32,'col_0'=8,'col_1'=2] {'row'}, dimensions={0} | all-to-all | bytes 393216 | tf_op jit(solution)/shard_map/all_to_all | solution.py:49
  137.0 15.6 %all_to_all.30 = bf16[32,24,128]{2,1,0:T(8,128)(2,1)} all-to-all(bf16[32,24,128]{2,1,0:T(8,128)(2,1)S(1)} %broadcast_in_dim.15), channel_id=1, replica_groups=mesh['row'=32,'col_0'=8,'col_1'=2] {'row'}, dimensions={0} | all-to-all | bytes 393216 | tf_op jit(solution)/shard_map/all_to_all | solution.py:26
  152.6 0.0 all-gather.2.cloned.1.call-update
  152.6 99.3 %all-gather.2.cloned.1.call-done = bf16[12,64,2048]{2,1,0:T(8,128)(2,1)} async-done(((bf16[12,64,128]{2,1,0:T(8,128)(2,1)}), bf16[12,64,2048]{2,1,0:T(8,128)(2,1)}) %all-gather.2.cloned.1.call-update) | async-done | bytes 3145744 | tf_op jit(solution)/shard_map/all_gather | solution.py:86
  251.9 0.0 copy-done
  251.9 3.7 %fusion.9 = bf16[2048,512]{1,0:T(8,128)(2,1)S(1)} fusion(bf16[12,64,2048]{2,1,0:T(8,128)(2,1)} %all-gather.2.cloned.1.call-done, bf16[12,64,512]{2,1,0:T(8,128)(2,1)S(1)} %copy-done), kind=kOutput, calls=%fused_computation.11 | convolution fusion | flops 1612709888 | bytes 6029312 | tf_op jit(solution)/shard_map/tsc,tsp->cp/dot_general | solution.py:84
  255.7 52.2 %all_to_all.31 = bf16[16,128,512]{2,1,0:T(8,128)(2,1)S(1)} all-to-all(bf16[16,128,512]{2,1,0:T(8,128)(2,1)S(1)} %bitcast.30), channel_id=1, replica_groups=mesh['row'=32,'col_0'=8,'col_1'=2] {'col_0','col_1'}, dimensions={0} | all-to-all | bytes 4194304 | tf_op jit(solution)/shard_map/all_to_all | solution.py:91
  307.9 1.5 copy.7
  (15 shorter events, 0.2 us)
Async XLA Ops:
  6.5 85.4 %reduce-scatter.5.cloned.1.call-start = ((), (), s32[]{:S(2)}) async-start(), calls=%async_computation.5 | async-start | bytes 3538944 | tf_op jit(solution)/shard_map/reduce_scatter | solution.py:13
  37.1 214.8 %copy-start = (bf16[12,64,512]{2,1,0:T(8,128)(2,1)S(1)}, bf16[12,64,512]{2,1,0:T(8,128)(2,1)}, u32[]{:S(2)}) copy-start(bf16[12,64,512]{2,1,0:T(8,128)(2,1)} %get-tuple-element.103) | copy-start | bytes 2359300
  37.1 77.8 %reduce-scatter.7.cloned.1.call-start = ((), (), s32[]{:S(2)}) async-start(), calls=%async_computation.7 | async-start | bytes 589824
  95.2 156.7 %all-gather.2.cloned.1.call-start = ((), (), s32[]{:S(2)}) async-start(), calls=%async_computation.6 | async-start | bytes 3342336 | tf_op jit(solution)/shard_map/all_gather | solution.py:86
Sparse Core Ops, SparseCore 0:
  37.2 54.6 reduce-scatter.4
  95.4 19.4 reduce-scatter.6
  152.8 99.1 all-gather.1
where the time goes:
time: 317 us; the launch traced here: 316 us
  waiting for transfers between devices  174 us (55%)
  blocking collectives  88.2 us (28%)
  matrix products  33.2 us (10%)
  between operations  13.2 us (4%)
  local copies, waits for them, and re-layouts  6.65 us (2%)
    all_gather x1, waiting for transfers between devices, body(): lax.all_gather(readings, COL, axis=2, tiled=True)  99.3 us
    reduce_scatter x1, waiting for transfers between devices, scatter_axes(): value = lax.psum_scatter(value, axis, scatter_dimension=dim, tiled=True)  54.7 us
    all_to_all x1, blocking collectives, body(): return lax.all_to_all(rounded, COL, split_axis=0, concat_axis=1, tiled=True)  52.2 us
    dot_general x12, matrix products, one_tier(): return jnp.dot(tier_fields, selector, preferred_element_type=jnp.float32)  29.5 us
    all_to_all x1, blocking collectives, sent_and_summed(): lax.all_to_all(blocks, axis, split_axis=0, concat_axis=0, tiled=True)  20.3 us
    unnamed x4, waiting for transfers between devices  19.7 us
    all_to_all x1, blocking collectives, sent_to_all(): lax.all_to_all(jnp.broadcast_to(value[None], (length, *value.shape)), axi...  15.6 us
  transfers between devices with their start and end apart: 3, of which 3 were waited for; matrix products, arithmetic and copies ran while one was open for 0% of the time, Pallas kernels for 0%

commit v1 on v0

--- a/solution.py
+++ b/solution.py
@@ -83,7 +83,9 @@
     scale_factor = 1.0 / jnp.sqrt(jnp.float32(temps.shape[0] * temps.shape[1]))
     summed = jnp.einsum(
         "tsc,tsp->cp",
-        lax.all_gather(readings, COL, axis=2, tiled=True),
+        jnp.concatenate(
+            lax.all_to_all(jnp.stack([readings] * lax.axis_size(COL)), COL, 0, 0), axis=2
+        ),
         temps,
         preferred_element_type=jnp.float32,
     )

time: 317 us -> 300 us (0.946)
  the two profiles are of different devices: /device:TPU:4 before, /device:TPU:16 now
where the time goes in v1:
time: 300 us; the launch traced here: 299 us
  blocking collectives  171 us (57%)
  waiting for transfers between devices  74.6 us (25%)
  matrix products  31.4 us (10%)
  between operations  13.5 us (4%)
  local copies, waits for them, and re-layouts  7.43 us (2%)
    all_to_all x1, blocking collectives, body(): lax.all_to_all(jnp.stack([readings] * lax.axis_size(COL)), COL, 0, 0)  81 us
    reduce_scatter x1, waiting for transfers between devices, scatter_axes(): value = lax.psum_scatter(value, axis, scatter_dimension=dim, tiled=True)  54.7 us
    all_to_all x1, blocking collectives, body(): return lax.all_to_all(rounded, COL, split_axis=0, concat_axis=1, tiled=True)  54.2 us
    dot_general x12, matrix products, one_tier(): return jnp.dot(tier_fields, selector, preferred_element_type=jnp.float32)  29.5 us
    all_to_all x1, blocking collectives, sent_and_summed(): lax.all_to_all(blocks, axis, split_axis=0, concat_axis=0, tiled=True)  20.3 us
    unnamed x3, waiting for transfers between devices  19.9 us
    all_to_all x1, blocking collectives, sent_to_all(): lax.all_to_all(jnp.broadcast_to(value[None], (length, *value.shape)), axi...  15.5 us
  transfers between devices with their start and end apart: 2, of which 2 were waited for; matrix products, arithmetic and copies ran while one was open for 0% of the time, Pallas kernels for 0%

profile of v1, /device:TPU:16, one launch (start us, length us, event | category | flops | bytes accessed | tf_op | source)
XLA Modules:
  0.0 298.8 jit_solution(1203254065565712150)
XLA Ops:
  6.5 0.0 reduce-scatter.5.cloned.1.call-start
  6.5 0.9 broadcast_subtract_fusion
  7.5 29.7 %while.11 = (s32[]{:T(128)}, bf16[12,64,2048]{2,1,0:T(8,128)(2,1)}, bf16[12,64,512]{2,1,0:T(8,128)(2,1)}, s32[12,2048]{1,0:T(8,128)S(1)}, s32[]{:T(128)}) while((s32[]{:T(128)}, bf16[12,64,2048]{2,1,0:T(8,128)(2,1)}, bf16[12,64,512]{2,1,0:T(8,128)(2,1)}, s32[12,2048]{1,0:T(8,128)S(1)}, s32[]{:T(128)}) %tuple.21), condition=%wide.region_1.2_spmd.clone, body=%wide.region_0.1_spmd.clone.sunk | while | flops 135266304 | bytes 615489 | solution.py:70
  7.5 2.4 fusion.17
  9.9 2.4 fusion.17
  12.4 2.5 fusion.17
  14.9 2.5 fusion.17
  17.4 2.5 fusion.17
  19.8 2.5 fusion.17
  22.3 2.5 fusion.17
  24.8 2.5 fusion.17
  27.3 2.5 fusion.17
  29.8 2.5 fusion.17
  32.2 2.5 fusion.17
  34.7 2.5 fusion.17
  37.2 0.0 reduce-scatter.5.cloned.1.call-update
  37.2 0.0 reduce-scatter.7.cloned.1.call-start
  37.2 54.7 %reduce-scatter.5.cloned.1.call-done = bf16[12,64,256]{2,1,0:T(8,128)(2,1)} async-done(((bf16[12,64,2048]{2,1,0:T(8,128)(2,1)}), bf16[12,64,256]{2,1,0:T(8,128)(2,1)}) %reduce-scatter.5.cloned.1.call-update) | async-done | bytes 393232 | tf_op jit(solution)/shard_map/reduce_scatter | solution.py:13
  91.9 1.9 copy.6
  93.9 1.4 reshape.16
  95.2 0.0 reduce-scatter.7.cloned.1.call-update
  95.3 19.8 %reduce-scatter.7.cloned.1.call-done = bf16[128,768]{1,0:T(8,128)(2,1)} async-done(((bf16[256,768]{1,0:T(8,128)(2,1)}), bf16[128,768]{1,0:T(8,128)(2,1)}) %reduce-scatter.7.cloned.1.call-update) | async-done | bytes 196624
  115.1 1.3 reshape.17
  116.4 0.4 copy.7
  116.7 20.3 %all_to_all.34 = bf16[32,24,128]{2,1,0:T(8,128)(2,1)S(1)} all-to-all(bf16[32,24,128]{2,1,0:T(8,128)(2,1)S(1)} %bitcast.40), channel_id=1, replica_groups=mesh['row'=32,'col_0'=8,'col_1'=2] {'row'}, dimensions={0} | all-to-all | bytes 393216 | tf_op jit(solution)/shard_map/all_to_all | solution.py:49
  137.1 15.5 %all_to_all.35 = bf16[32,24,128]{2,1,0:T(8,128)(2,1)S(1)} all-to-all(bf16[32,24,128]{2,1,0:T(8,128)(2,1)S(1)} %broadcast_in_dim.15), channel_id=1, replica_groups=mesh['row'=32,'col_0'=8,'col_1'=2] {'row'}, dimensions={0} | all-to-all | bytes 393216 | tf_op jit(solution)/shard_map/all_to_all | solution.py:26
  152.6 0.8 stack.5
  153.4 0.0 copy-start
  153.4 81.0 %all_to_all.36 = bf16[16,12,64,128]{3,2,1,0:T(8,128)(2,1)S(1)} all-to-all(bf16[16,12,64,128]{3,2,1,0:T(8,128)(2,1)S(1)} %stack.5), channel_id=1, replica_groups=mesh['row'=32,'col_0'=8,'col_1'=2] {'col_0','col_1'}, dimensions={0} | all-to-all | bytes 6291456 | tf_op jit(solution)/shard_map/all_to_all | solution.py:87
  234.4 0.0 copy-done
  234.4 1.8 fusion.9
  236.2 54.2 %all_to_all.37 = bf16[16,128,512]{2,1,0:T(8,128)(2,1)S(1)} all-to-all(bf16[16,128,512]{2,1,0:T(8,128)(2,1)S(1)} %bitcast.37), channel_id=1, replica_groups=mesh['row'=32,'col_0'=8,'col_1'=2] {'col_0','col_1'}, dimensions={0} | all-to-all | bytes 4194304 | tf_op jit(solution)/shard_map/all_to_all | solution.py:93
  290.4 1.5 copy.9
  (15 shorter events, 0.2 us)
Async XLA Ops:
  6.5 85.4 %reduce-scatter.5.cloned.1.call-start = ((), (), s32[]{:S(2)}) async-start(), calls=%async_computation.6 | async-start | bytes 3538944 | tf_op jit(solution)/shard_map/reduce_scatter | solution.py:13
  37.2 77.9 %reduce-scatter.7.cloned.1.call-start = ((), (), s32[]{:S(2)}) async-start(), calls=%async_computation.7 | async-start | bytes 589824
  153.4 81.0 %copy-start = (bf16[12,64,512]{2,1,0:T(8,128)(2,1)S(1)}, bf16[12,64,512]{2,1,0:T(8,128)(2,1)}, u32[]{:S(2)}) copy-start(bf16[12,64,512]{2,1,0:T(8,128)(2,1)} %get-tuple-element.99) | copy-start | bytes 2359300
Sparse Core Ops, SparseCore 0:
  37.3 54.5 reduce-scatter.4
  95.4 19.6 reduce-scatter.6
